TPU v7x, 128 devices: a whole 4x4x4 slice. The times are simulated.
128 devices in a mesh: blk: 8 (over y, z_lo), mode: 16 (over z_hi, x, core).
Axes of the slice: x: 4, y: 4, z: 4 (z_hi: 2, z_lo: 2; z = z_hi * 2 + z_lo), core: 2. Of those that a mesh axis runs over, the one named last changes fastest.
Arguments:
- density: bfloat16 [2, 256, 2048, 256], P(None, 'mode', 'blk'), may hold values from -6 to 6
- kernel_tiles: bfloat16 [256, 16, 8, 2, 128, 128], P('mode', 'blk'), may hold values from -0.125 to 0.125
- tile_index: int32 [256, 16, 8], P('mode', 'blk'), may hold values from 0 to 1
- coupling: bfloat16 [2, 9, 256, 2048], P(None, None, 'mode', 'blk'), may hold values from -4 to 4
- spread: int32 [2048], P('blk'), may hold values from 0 to 4
- liner: int32 [2048], P('blk'), may hold values 0 or 1
Outputs:
- applied: bfloat16 [2, 256, 2048, 256], P(None, 'mode', 'blk')
Inputs may be any that keep to these rules, and one draw needn't show every extreme that they name: `tile_index`: each retained tile names one column tile of its source shard.
All inputs are finite; a program needn't handle non-finite values. No bound on the sum of `liner` on one device may be relied on, other than what follows from the above.
Results may differ from a plain program's by a relative error of at most 0.0033.
Values may be sent and summed in bfloat16 or wider, within the bound.
No kernel may reach another device: no remote copies, remote signals or barrier semaphores. Data moves between devices by JAX's collectives and lax.ppermute only.
A program may use at most 320 MiB of HBM per device.

v0:
```python
import jax
import jax.numpy as jnp
from jax import lax
from jax.sharding import PartitionSpec as P


def with_halo(block, sides, width):
    for axis, dim in sides:
        count = lax.axis_size(axis)
        forward = [(i, i + 1) for i in range(count - 1)]
        backward = [(target, source) for source, target in forward]
        low = lax.ppermute(
            lax.slice_in_dim(block, block.shape[dim] - width, None, axis=dim), axis, forward
        )
        high = lax.ppermute(lax.slice_in_dim(block, 0, width, axis=dim), axis, backward)
        block = jnp.concatenate([low, block, high], axis=dim)
    return block


def tile_product(left, right):
    return jnp.einsum("mtqk,mtkr->mtqr", left, right, preferred_element_type=jnp.float32)


def couple_modes(padded, weights, mode_count):
    band_count = weights.shape[1]
    real_part = jnp.zeros((mode_count,) + padded.shape[2:], jnp.float32)
    imag_part = jnp.zeros((mode_count,) + padded.shape[2:], jnp.float32)
    for offset in range(band_count):
        shifted = padded[:, offset : offset + mode_count].astype(jnp.float32)
        weight_now = weights[:, offset].astype(jnp.float32)[..., None]
        real_part = real_part + weight_now[0] * shifted[0] - weight_now[1] * shifted[1]
        imag_part = imag_part + weight_now[0] * shifted[1] + weight_now[1] * shifted[0]
    return jnp.stack([real_part, imag_part]).astype(jnp.bfloat16)


def shards(density, kernel_tiles, tile_index, coupling, spread, liner):
    mode_count = density.shape[1]
    point_count = density.shape[2]
    rhs_count = density.shape[3]
    tile_size = kernel_tiles.shape[-1]
    row_tiles = kernel_tiles.shape[1]
    per_shard = point_count // tile_size
    band_count = coupling.shape[1]
    reach = band_count // 2
    column_ids = jnp.arange(per_shard, dtype=jnp.int32)
    initial = jnp.zeros((2, mode_count, row_tiles, tile_size, rhs_count), jnp.float32)
    gathered = lax.all_gather(density, "blk", axis=2, tiled=True)
    shard_count = gathered.shape[2] // point_count

    def one_shard(position, running):
        shard_block = lax.dynamic_slice_in_dim(gathered, position * point_count, point_count, 2)
        shard_block = shard_block.reshape(2, mode_count, per_shard, tile_size, rhs_count)
        chosen_tiles = lax.dynamic_index_in_dim(tile_index, position, 2, keepdims=False)
        one_hot = (chosen_tiles[:, :, None] == column_ids).astype(jnp.bfloat16)
        picked_tiles = jnp.einsum(
            "mts,cmsqr->cmtqr", one_hot, shard_block, preferred_element_type=jnp.float32
        ).astype(jnp.bfloat16)
        kernel_block = lax.dynamic_index_in_dim(kernel_tiles, position, 2, keepdims=False)
        real_part = tile_product(kernel_block[:, :, 0], picked_tiles[0]) - tile_product(
            kernel_block[:, :, 1], picked_tiles[1]
        )
        imag_part = tile_product(kernel_block[:, :, 0], picked_tiles[1]) + tile_product(
            kernel_block[:, :, 1], picked_tiles[0]
        )
        return running + jnp.stack([real_part, imag_part])

    near = lax.fori_loop(0, shard_count, one_shard, initial)
    near = near.reshape(2, mode_count, point_count, rhs_count)
    offsets = jnp.abs(jnp.arange(band_count, dtype=jnp.int32) - reach)
    within = (offsets[:, None] <= spread[None, :]) & (liner[None, :] == 1)
    weights = coupling * within[None, :, None, :].astype(jnp.bfloat16)
    extended = with_halo(density, (("mode", 1),), reach)
    coupled = couple_modes(extended, weights, mode_count)
    total = 0.5 * density.astype(jnp.float32) + near + coupled.astype(jnp.float32)
    return total.astype(jnp.bfloat16)


def solution(mesh):
    return jax.shard_map(
        shards,
        mesh=mesh,
        in_specs=(
            P(None, "mode", "blk", None),
            P("mode", "blk", None, None, None, None),
            P("mode", "blk", None),
            P(None, None, "mode", "blk"),
            P("blk"),
            P("blk"),
        ),
        out_specs=P(None, "mode", "blk", None),
        check_vma=False,
    )
```

profile of v0, /device:TPU:1, one launch (start us, length us, event | category | flops | bytes accessed | tf_op | source)
XLA Modules:
  0.0 1023.9 jit_solution(228144644666771216)
XLA Ops:
  17.0 9.9 collective-permute-done
  26.9 7.9 constant_dynamic-update-slice_fusion
  37.2 11.7 %slice_convert_fusion.3 = (f32[2,16,256,256]{3,2,1,0:T(8,128)}, f32[2,16,256,256]{3,2,1,0:T(8,128)}, f32[2,16,256,256]{3,2,1,0:T(8,128)}, f32[2,16,256,256]{3,2,1,0:T(8,128)}) fusion(bf16[2,20,256,256]{3,2,1,0:T(8,128)(2,1)S(1)} %constant_dynamic-update-slice_fusion.2), kind=kLoop, calls=%fused_computation.30 | loop fusion | flops 8388608 | bytes 50331648 | tf_op jit(solution)/shard_map/convert_element_type | solution.py:29
  48.9 15.3 %slice_convert_fusion.7 = (f32[2,16,256,256]{3,2,1,0:T(8,128)}, f32[2,16,256,256]{3,2,1,0:T(8,128)}, f32[2,16,256,256]{3,2,1,0:T(8,128)}, f32[2,16,256,256]{3,2,1,0:T(8,128)}) fusion(bf16[2,20,256,256]{3,2,1,0:T(8,128)(2,1)} %copy-done), kind=kLoop, calls=%fused_computation.34 | loop fusion | flops 8388608 | bytes 50331648 | tf_op jit(solution)/shard_map/convert_element_type | solution.py:29
  64.2 24.6 %subtract_convert_fusion = bf16[1,16,256,256]{3,2,1,0:T(8,128)(2,1)} fusion(f32[2,16,256,256]{3,2,1,0:T(8,128)} %get-tuple-element.162, f32[2,16,256,256]{3,2,1,0:T(8,128)} %get-tuple-element.163, f32[2,16,256,256]{3,2,1,0:T(8,128)} %get-tuple-element.164, f32[2,16,256,256]{3,2,1,0:T(8,128)} %get-tuple-element.161, ...), kind=kLoop, calls=%fused_computation.36 | loop fusion | flops 37748736 | bytes 77889536 | tf_op jit(solution)/shard_map/convert
  88.8 25.0 %add_convert_fusion = bf16[1,16,256,256]{3,2,1,0:T(8,128)(2,1)} fusion(f32[2,16,256,256]{3,2,1,0:T(8,128)} %get-tuple-element.162, f32[2,16,256,256]{3,2,1,0:T(8,128)} %get-tuple-element.163, f32[2,16,256,256]{3,2,1,0:T(8,128)} %get-tuple-element.164, f32[2,16,256,256]{3,2,1,0:T(8,128)} %get-tuple-element.161, f32[2,16,256,256]{3,2,1,0:T(8,128)} %get-tuple-element.166, ...), kind=kLoop, calls=%fused_computation.35 | loop fusion | flops 37748736 | bytes 77889536 | tf_op jit(solution)/shard_map/convert.1
  113.8 548.6 %all-gather.2.cloned.1.call-done = bf16[2,16,2048,256]{3,2,1,0:T(8,128)(2,1)} async-done(((bf16[2,16,256,256]{3,2,1,0:T(8,128)(2,1)}), bf16[2,16,2048,256]{3,2,1,0:T(8,128)(2,1)}) %all-gather.2.cloned.1.call-update) | async-done | bytes 33554448 | tf_op jit(solution)/shard_map/all_gather | solution.py:47
  662.4 346.8 %while.14 = (s32[]{:T(128)}, f32[2,16,2,128,256]{4,3,2,1,0:T(8,128)}, bf16[16,2,8,2,128,128]{5,4,3,2,1,0:T(8,128)(2,1)}, bf16[2,16,2048,256]{3,2,1,0:T(8,128)(2,...) while((s32[]{:T(128)}, f32[2,16,2,128,256]{4,3,2,1,0:T(8,128)}, ...), condition=%wide.region_1.2_spmd.clone, body=%wide.region_0.1_spmd.clone.sunk | while | flops 1092616192 | bytes 92275992 | solution.py:67
  667.9 16.7 %fusion.28 = bf16[2,16,2,128,256]{4,2,3,0,1:T(2,128)(2,1)S(1)} fusion(bf16[2,16,2,128,256]{4,3,2,1,0:T(8,128)(2,1)} %bitcast.95, s32[16,2]{1,0:T(8,128)S(1)} %copy.49), kind=kOutput, calls=%fused_computation.3.clone.1 | convolution fusion | flops 10485824 | bytes 8388736 | tf_op jit(solution)/shard_map/while/body/eval_jaxpr/mts,cmsqr->cmtqr/dot_general | solution.py:55
  707.9 16.7 %fusion.28 = bf16[2,16,2,128,256]{4,2,3,0,1:T(2,128)(2,1)S(1)} fusion(bf16[2,16,2,128,256]{4,3,2,1,0:T(8,128)(2,1)} %bitcast.95, s32[16,2]{1,0:T(8,128)S(1)} %copy.49), kind=kOutput, calls=%fused_computation.3.clone.1 | convolution fusion | flops 10485824 | bytes 8388736 | tf_op jit(solution)/shard_map/while/body/eval_jaxpr/mts,cmsqr->cmtqr/dot_general | solution.py:55
  736.2 10.1 maximum_add_fusion.2
  751.7 16.7 %fusion.28 = bf16[2,16,2,128,256]{4,2,3,0,1:T(2,128)(2,1)S(1)} fusion(bf16[2,16,2,128,256]{4,3,2,1,0:T(8,128)(2,1)} %bitcast.95, s32[16,2]{1,0:T(8,128)S(1)} %copy.49), kind=kOutput, calls=%fused_computation.3.clone.1 | convolution fusion | flops 10485824 | bytes 8388736 | tf_op jit(solution)/shard_map/while/body/eval_jaxpr/mts,cmsqr->cmtqr/dot_general | solution.py:55
  780.1 10.1 maximum_add_fusion.2
  795.6 16.7 %fusion.28 = bf16[2,16,2,128,256]{4,2,3,0,1:T(2,128)(2,1)S(1)} fusion(bf16[2,16,2,128,256]{4,3,2,1,0:T(8,128)(2,1)} %bitcast.95, s32[16,2]{1,0:T(8,128)S(1)} %copy.49), kind=kOutput, calls=%fused_computation.3.clone.1 | convolution fusion | flops 10485824 | bytes 8388736 | tf_op jit(solution)/shard_map/while/body/eval_jaxpr/mts,cmsqr->cmtqr/dot_general | solution.py:55
  823.9 10.1 maximum_add_fusion.2
  839.4 16.7 %fusion.28 = bf16[2,16,2,128,256]{4,2,3,0,1:T(2,128)(2,1)S(1)} fusion(bf16[2,16,2,128,256]{4,3,2,1,0:T(8,128)(2,1)} %bitcast.95, s32[16,2]{1,0:T(8,128)S(1)} %copy.49), kind=kOutput, calls=%fused_computation.3.clone.1 | convolution fusion | flops 10485824 | bytes 8388736 | tf_op jit(solution)/shard_map/while/body/eval_jaxpr/mts,cmsqr->cmtqr/dot_general | solution.py:55
  867.7 10.1 maximum_add_fusion.2
  883.2 16.7 %fusion.28 = bf16[2,16,2,128,256]{4,2,3,0,1:T(2,128)(2,1)S(1)} fusion(bf16[2,16,2,128,256]{4,3,2,1,0:T(8,128)(2,1)} %bitcast.95, s32[16,2]{1,0:T(8,128)S(1)} %copy.49), kind=kOutput, calls=%fused_computation.3.clone.1 | convolution fusion | flops 10485824 | bytes 8388736 | tf_op jit(solution)/shard_map/while/body/eval_jaxpr/mts,cmsqr->cmtqr/dot_general | solution.py:55
  911.5 10.1 maximum_add_fusion.2
  927.0 16.7 %fusion.28 = bf16[2,16,2,128,256]{4,2,3,0,1:T(2,128)(2,1)S(1)} fusion(bf16[2,16,2,128,256]{4,3,2,1,0:T(8,128)(2,1)} %bitcast.95, s32[16,2]{1,0:T(8,128)S(1)} %copy.49), kind=kOutput, calls=%fused_computation.3.clone.1 | convolution fusion | flops 10485824 | bytes 8388736 | tf_op jit(solution)/shard_map/while/body/eval_jaxpr/mts,cmsqr->cmtqr/dot_general | solution.py:55
  955.3 10.1 maximum_add_fusion.2
  970.8 16.7 %fusion.28 = bf16[2,16,2,128,256]{4,2,3,0,1:T(2,128)(2,1)S(1)} fusion(bf16[2,16,2,128,256]{4,3,2,1,0:T(8,128)(2,1)} %bitcast.95, s32[16,2]{1,0:T(8,128)S(1)} %copy.49), kind=kOutput, calls=%fused_computation.3.clone.1 | convolution fusion | flops 10485824 | bytes 8388736 | tf_op jit(solution)/shard_map/while/body/eval_jaxpr/mts,cmsqr->cmtqr/dot_general | solution.py:55
  999.1 10.1 maximum_add_fusion.2
  1009.2 7.8 fusion.13
  (102 shorter events, 155.0 us)
Async XLA Ops:
  6.5 10.2 %copy-start.4 = (s32[256]{0:T(256)S(1)}, s32[256]{0:T(256)}, u32[]{:S(2)}) copy-start(s32[256]{0:T(256)} %param.13) | copy-start | bytes 3076
  6.5 10.3 %copy-start.3 = (s32[256]{0:T(256)S(1)}, s32[256]{0:T(256)}, u32[]{:S(2)}) copy-start(s32[256]{0:T(256)} %param.12) | copy-start | bytes 3076
  6.5 10.4 %copy-start.2 = (bf16[2,9,16,256]{3,2,1,0:T(8,128)(2,1)S(1)}, bf16[2,9,16,256]{3,2,1,0:T(8,128)(2,1)}, u32[]{:S(2)}) copy-start(bf16[2,9,16,256]{3,2,1,0:T(8,128)(2,1)} %param.11) | copy-start | bytes 442372
  6.5 655.8 %all-gather.2.cloned.1.call-start = ((), (), s32[]{:S(2)}) async-start(), calls=%async_computation | async-start | bytes 37748736 | tf_op jit(solution)/shard_map/all_gather | solution.py:47
  10.3 16.5 %collective-permute-start = (bf16[2,4,256,256]{3,2,1,0:T(8,128)(2,1)}, bf16[2,4,256,256]{3,2,1,0:T(8,128)(2,1)S(1)}, u32[]{:S(2)}, u32[]{:S(2)}) collective-permute-start(bf16[2,4,256,256]{3,2,1,0:T(8,128)(2,1)} %get-tuple-element.168), channel_id=1, source_target_pairs={{0,1},{1,2},{2,3},{3,4},{4,5},{5,6},{6,7},{7,8},{8,9},{9,10},{10,1... | collective-permute-start | bytes 3145736 | tf_op jit(solution)/shard_map/ppermute | solution.py:12
  14.8 20.1 %collective-permute-start.1 = (bf16[2,4,256,256]{3,2,1,0:T(8,128)(2,1)}, bf16[2,4,256,256]{3,2,1,0:T(8,128)(2,1)S(1)}, u32[]{:S(2)}, u32[]{:S(2)}) collective-permute-start(bf16[2,4,256,256]{3,2,1,0:T(8,128)(2,1)} %get-tuple-element.169), channel_id=1, source_target_pairs={{1,0},{2,1},{3,2},{4,3},{5,4},{6,5},{7,6},{8,7},{9,8},{10,9},{11,1... | collective-permute-start | bytes 3145736 | tf_op jit(solution)/shard_map/ppermute | solution.py:15
  34.9 2.3 copy-start
  662.4 346.8 %copy-start.1 = (bf16[1,16,256,256]{3,2,1,0:T(8,128)(2,1)S(1)}, bf16[1,16,256,256]{3,2,1,0:T(8,128)(2,1)}, u32[]{:S(2)}) copy-start(bf16[1,16,256,256]{3,2,1,0:T(8,128)(2,1)} %subtract_convert_fusion) | copy-start | bytes 6291460
Sparse Core Ops, SparseCore 0:
  9.0 653.3 all-gather.1
where the time goes:
time: 1020 us
  waiting for transfers between devices  559 us (55%)
  matrix products  188 us (18%)
  other arithmetic  169 us (17%)
  local copies, waits for them, and re-layouts  87.5 us (9%)
  between operations  13.5 us (1%)
    all_gather x1, waiting for transfers between devices, shards(): gathered = lax.all_gather(density, 'blk', axis=2, tiled=True)  549 us
    dot_general x8, matrix products, one_shard(): jnp.einsum('mts,cmsqr->cmtqr', one_hot, shard_block, preferred_element_ty...  134 us
    add x8, other arithmetic, one_shard(): return running + jnp.stack([real_part, imag_part])  76.8 us
    dot_general x32, matrix products, tile_product(): jnp.einsum('mtqk,mtkr->mtqr', left, right, preferred_element_type=jnp.flo...  54 us
    another operation x2, other arithmetic  49.6 us
    dynamic_slice x8, local copies, waits for them, and re-layouts, one_shard(): lax.dynamic_slice_in_dim(gathered, position * point_count, point_count, 2)  37.3 us
    convert_element_type x2, other arithmetic, couple_modes(): shifted = padded[:, offset:offset + mode_count].astype(jnp.float32)  27 us
    squeeze x8, local copies, waits for them, and re-layouts, one_shard(): picked_tiles[0]  23.6 us
  transfers between devices with their start and end apart: 3, of which 2 were waited for; matrix products, arithmetic and copies ran while one was open for 9% of the time, Pallas kernels for 0%

commit v1 on v0

--- a/solution.py
+++ b/solution.py
@@ -44,7 +44,9 @@
     reach = band_count // 2
     column_ids = jnp.arange(per_shard, dtype=jnp.int32)
     initial = jnp.zeros((2, mode_count, row_tiles, tile_size, rhs_count), jnp.float32)
-    gathered = lax.all_gather(density, "blk", axis=2, tiled=True)
+    gathered = jnp.concatenate(
+        lax.all_to_all(jnp.stack([density] * lax.axis_size("blk")), "blk", 0, 0), axis=2
+    )
     shard_count = gathered.shape[2] // point_count
 
     def one_shard(position, running):

time: 1020 us -> 863 us (0.85)
  waiting for transfers between devices: 559 us -> 367 us
  local copies, waits for them, and re-layouts: 87.5 us -> 123 us
  between operations: 13.5 us -> 0.16 us
    all_gather x1 -> x0, waiting for transfers between devices: 549 us -> none  [shards(): gathered = lax.all_gather(density, 'blk', axis=2, tiled=True)]
    all_to_all x0 -> x1, waiting for transfers between devices: none -> 357 us  [shards(): lax.all_to_all(jnp.stack([density] * lax.axis_size('blk')), 'blk', 0, 0)]
    all_to_all x0 -> x1, local copies, waits for them, and re-layouts: none -> 23 us  [shards(): lax.all_to_all(jnp.stack([density] * lax.axis_size('blk')), 'blk', 0, 0)]
    another operation x0 -> x1, local copies, waits for them, and re-layouts: none -> 12.4 us  [shards(): jnp.stack([density] * lax.axis_size('blk'))]
  transfers between devices with their start and end apart: 3 -> 3, of which waited for: 2 -> 2; matrix products, arithmetic and copies ran while one was open for 9% -> 10% of each run, Pallas kernels for 0% -> 0%
where the time goes in v1:
time: 863 us; the launch traced here: 861 us
  waiting for transfers between devices  367 us (43%)
  matrix products  188 us (22%)
  other arithmetic  169 us (20%)
  local copies, waits for them, and re-layouts  123 us (14%)
  starting transfers between devices  13.5 us (2%)
    all_to_all x1, waiting for transfers between devices, shards(): lax.all_to_all(jnp.stack([density] * lax.axis_size('blk')), 'blk', 0, 0)  357 us
    dot_general x8, matrix products, one_shard(): jnp.einsum('mts,cmsqr->cmtqr', one_hot, shard_block, preferred_element_ty...  134 us
    add x8, other arithmetic, one_shard(): return running + jnp.stack([real_part, imag_part])  76.6 us
    dot_general x32, matrix products, tile_product(): jnp.einsum('mtqk,mtkr->mtqr', left, right, preferred_element_type=jnp.flo...  54.2 us
    another operation x2, other arithmetic  49.2 us
    dynamic_slice x8, local copies, waits for them, and re-layouts, one_shard(): lax.dynamic_slice_in_dim(gathered, position * point_count, point_count, 2)  37.3 us
    convert_element_type x2, other arithmetic, couple_modes(): shifted = padded[:, offset:offset + mode_count].astype(jnp.float32)  27 us
    squeeze x8, local copies, waits for them, and re-layouts, one_shard(): picked_tiles[0]  23.6 us
  transfers between devices with their start and end apart: 3, of which 2 were waited for; matrix products, arithmetic and copies ran while one was open for 10% of the time, Pallas kernels for 0%

profile of v1, /device:TPU:1, one launch (start us, length us, event | category | flops | bytes accessed | tf_op | source)
XLA Modules:
  0.0 860.8 jit_solution(11411039987848181569)
XLA Ops:
  0.0 12.4 %stack.38 = bf16[8,2,16,256,256]{4,3,2,1,0:T(8,128)(2,1)} broadcast(bf16[2,16,256,256]{3,2,1,0:T(8,128)(2,1)} %param.8), dimensions={1,2,3,4} | broadcast | bytes 37748736 | tf_op jit(solution)/shard_map/stack | solution.py:48
  29.3 9.9 %collective-permute-done = bf16[2,4,256,256]{3,2,1,0:T(8,128)(2,1)S(1)} collective-permute-done((bf16[2,4,256,256]{3,2,1,0:T(8,128)(2,1)}, bf16[2,4,256,256]{3,2,1,0:T(8,128)(2,1)S(1)}, u32[]{:S(2)}, u32[]{:S(2)}) %collective-permute-start) | collective-permute-done | bytes 1048608 | tf_op jit(solution)/shard_map/ppermute | solution.py:12
  49.6 11.7 %slice_convert_fusion.3 = (f32[2,16,256,256]{3,2,1,0:T(8,128)}, f32[2,16,256,256]{3,2,1,0:T(8,128)}, f32[2,16,256,256]{3,2,1,0:T(8,128)}, f32[2,16,256,256]{3,2,1,0:T(8,128)}) fusion(bf16[2,20,256,256]{3,2,1,0:T(8,128)(2,1)S(1)} %constant_dynamic-update-slice_fusion.2), kind=kLoop, calls=%fused_computation.30 | loop fusion | flops 8388608 | bytes 50331648 | tf_op jit(solution)/shard_map/convert_element_type | solution.py:29
  61.3 15.2 %slice_convert_fusion.7 = (f32[2,16,256,256]{3,2,1,0:T(8,128)}, f32[2,16,256,256]{3,2,1,0:T(8,128)}, f32[2,16,256,256]{3,2,1,0:T(8,128)}, f32[2,16,256,256]{3,2,1,0:T(8,128)}) fusion(bf16[2,20,256,256]{3,2,1,0:T(8,128)(2,1)} %copy-done), kind=kLoop, calls=%fused_computation.34 | loop fusion | flops 8388608 | bytes 50331648 | tf_op jit(solution)/shard_map/convert_element_type | solution.py:29
  76.6 24.6 %subtract_convert_fusion = bf16[1,16,256,256]{3,2,1,0:T(8,128)(2,1)} fusion(f32[2,16,256,256]{3,2,1,0:T(8,128)} %get-tuple-element.172, f32[2,16,256,256]{3,2,1,0:T(8,128)} %get-tuple-element.173, f32[2,16,256,256]{3,2,1,0:T(8,128)} %get-tuple-element.174, f32[2,16,256,256]{3,2,1,0:T(8,128)} %get-tuple-element.171, ...), kind=kLoop, calls=%fused_computation.36 | loop fusion | flops 37748736 | bytes 77889536 | tf_op jit(solution)/shard_map/convert
  101.2 24.6 %add_convert_fusion = bf16[1,16,256,256]{3,2,1,0:T(8,128)(2,1)} fusion(f32[2,16,256,256]{3,2,1,0:T(8,128)} %get-tuple-element.172, f32[2,16,256,256]{3,2,1,0:T(8,128)} %get-tuple-element.173, f32[2,16,256,256]{3,2,1,0:T(8,128)} %get-tuple-element.174, f32[2,16,256,256]{3,2,1,0:T(8,128)} %get-tuple-element.171, f32[2,16,256,256]{3,2,1,0:T(8,128)} %get-tuple-element.176, ...), kind=kLoop, calls=%fused_computation.35 | loop fusion | flops 37748736 | bytes 77889536 | tf_op jit(solution)/shard_map/convert.1
  125.8 357.2 %all-to-all-done = bf16[8,2,16,256,256]{4,3,2,1,0:T(8,128)(2,1)} async-done(((bf16[8,2,16,256,256]{4,3,2,1,0:T(8,128)(2,1)}), bf16[8,2,16,256,256]{4,3,2,1,0:T(8,128)(2,1)}, u32[]{:S(2)}, u32[]{:S(2)}) %all-to-all-start) | async-done | bytes 33554464 | tf_op jit(solution)/shard_map/all_to_all | solution.py:48
  483.0 23.0 %copy.36 = bf16[8,2,16,256,256]{4,3,0,2,1:T(8,128)(2,1)} copy(bf16[8,2,16,256,256]{4,3,2,1,0:T(8,128)(2,1)} %all-to-all-done) | data formatting | bytes 67108864 | tf_op jit(solution)/shard_map/all_to_all | solution.py:48
  506.0 347.0 %while.14 = (s32[]{:T(128)}, f32[2,16,2,128,256]{4,3,2,1,0:T(8,128)}, bf16[16,2,8,2,128,128]{5,4,3,2,1,0:T(8,128)(2,1)}, bf16[2,16,2048,256]{3,2,1,0:T(8,128)(2,...) while((s32[]{:T(128)}, f32[2,16,2,128,256]{4,3,2,1,0:T(8,128)}, ...), condition=%wide.region_1.2_spmd.clone, body=%wide.region_0.1_spmd.clone.sunk | while | flops 1092616192 | bytes 92275992 | solution.py:69
  511.7 16.7 %fusion.28 = bf16[2,16,2,128,256]{4,2,3,0,1:T(2,128)(2,1)S(1)} fusion(bf16[2,16,2,128,256]{4,3,2,1,0:T(8,128)(2,1)} %bitcast.98, s32[16,2]{1,0:T(8,128)S(1)} %copy.66), kind=kOutput, calls=%fused_computation.3.clone.1 | convolution fusion | flops 10485824 | bytes 8388736 | tf_op jit(solution)/shard_map/while/body/eval_jaxpr/mts,cmsqr->cmtqr/dot_general | solution.py:57
  551.7 16.7 %fusion.28 = bf16[2,16,2,128,256]{4,2,3,0,1:T(2,128)(2,1)S(1)} fusion(bf16[2,16,2,128,256]{4,3,2,1,0:T(8,128)(2,1)} %bitcast.98, s32[16,2]{1,0:T(8,128)S(1)} %copy.66), kind=kOutput, calls=%fused_computation.3.clone.1 | convolution fusion | flops 10485824 | bytes 8388736 | tf_op jit(solution)/shard_map/while/body/eval_jaxpr/mts,cmsqr->cmtqr/dot_general | solution.py:57
  580.0 10.1 %maximum_add_fusion.2 = f32[2,16,2,128,256]{4,3,2,1,0:T(8,128)} fusion(f32[1,16,2,128,256]{4,3,2,1,0:T(8,128)} %add_bitcast_fusion.2, f32[1,16,2,128,256]{4,3,2,1,0:T(8,128)} %subtract_bitcast_fusion.2, f32[2,16,2,128,256]{4,3,2,1,0:T(8,128)} %get-tuple-element.260, pred[]{:T(512)S(6)} %compare.3), kind=kLoop, calls=%fused_computation.1.clone.1 | loop fusion | flops 6291456 | bytes 25165824 | tf_op jit(solution)/shard_map/while/body/eval_jaxpr/add | solution.py:67
  595.5 16.7 %fusion.28 = bf16[2,16,2,128,256]{4,2,3,0,1:T(2,128)(2,1)S(1)} fusion(bf16[2,16,2,128,256]{4,3,2,1,0:T(8,128)(2,1)} %bitcast.98, s32[16,2]{1,0:T(8,128)S(1)} %copy.66), kind=kOutput, calls=%fused_computation.3.clone.1 | convolution fusion | flops 10485824 | bytes 8388736 | tf_op jit(solution)/shard_map/while/body/eval_jaxpr/mts,cmsqr->cmtqr/dot_general | solution.py:57
  623.8 10.1 %maximum_add_fusion.2 = f32[2,16,2,128,256]{4,3,2,1,0:T(8,128)} fusion(f32[1,16,2,128,256]{4,3,2,1,0:T(8,128)} %add_bitcast_fusion.2, f32[1,16,2,128,256]{4,3,2,1,0:T(8,128)} %subtract_bitcast_fusion.2, f32[2,16,2,128,256]{4,3,2,1,0:T(8,128)} %get-tuple-element.260, pred[]{:T(512)S(6)} %compare.3), kind=kLoop, calls=%fused_computation.1.clone.1 | loop fusion | flops 6291456 | bytes 25165824 | tf_op jit(solution)/shard_map/while/body/eval_jaxpr/add | solution.py:67
  639.3 16.7 %fusion.28 = bf16[2,16,2,128,256]{4,2,3,0,1:T(2,128)(2,1)S(1)} fusion(bf16[2,16,2,128,256]{4,3,2,1,0:T(8,128)(2,1)} %bitcast.98, s32[16,2]{1,0:T(8,128)S(1)} %copy.66), kind=kOutput, calls=%fused_computation.3.clone.1 | convolution fusion | flops 10485824 | bytes 8388736 | tf_op jit(solution)/shard_map/while/body/eval_jaxpr/mts,cmsqr->cmtqr/dot_general | solution.py:57
  667.6 10.1 %maximum_add_fusion.2 = f32[2,16,2,128,256]{4,3,2,1,0:T(8,128)} fusion(f32[1,16,2,128,256]{4,3,2,1,0:T(8,128)} %add_bitcast_fusion.2, f32[1,16,2,128,256]{4,3,2,1,0:T(8,128)} %subtract_bitcast_fusion.2, f32[2,16,2,128,256]{4,3,2,1,0:T(8,128)} %get-tuple-element.260, pred[]{:T(512)S(6)} %compare.3), kind=kLoop, calls=%fused_computation.1.clone.1 | loop fusion | flops 6291456 | bytes 25165824 | tf_op jit(solution)/shard_map/while/body/eval_jaxpr/add | solution.py:67
  683.1 16.7 %fusion.28 = bf16[2,16,2,128,256]{4,2,3,0,1:T(2,128)(2,1)S(1)} fusion(bf16[2,16,2,128,256]{4,3,2,1,0:T(8,128)(2,1)} %bitcast.98, s32[16,2]{1,0:T(8,128)S(1)} %copy.66), kind=kOutput, calls=%fused_computation.3.clone.1 | convolution fusion | flops 10485824 | bytes 8388736 | tf_op jit(solution)/shard_map/while/body/eval_jaxpr/mts,cmsqr->cmtqr/dot_general | solution.py:57
  711.5 10.1 %maximum_add_fusion.2 = f32[2,16,2,128,256]{4,3,2,1,0:T(8,128)} fusion(f32[1,16,2,128,256]{4,3,2,1,0:T(8,128)} %add_bitcast_fusion.2, f32[1,16,2,128,256]{4,3,2,1,0:T(8,128)} %subtract_bitcast_fusion.2, f32[2,16,2,128,256]{4,3,2,1,0:T(8,128)} %get-tuple-element.260, pred[]{:T(512)S(6)} %compare.3), kind=kLoop, calls=%fused_computation.1.clone.1 | loop fusion | flops 6291456 | bytes 25165824 | tf_op jit(solution)/shard_map/while/body/eval_jaxpr/add | solution.py:67
  726.9 16.7 %fusion.28 = bf16[2,16,2,128,256]{4,2,3,0,1:T(2,128)(2,1)S(1)} fusion(bf16[2,16,2,128,256]{4,3,2,1,0:T(8,128)(2,1)} %bitcast.98, s32[16,2]{1,0:T(8,128)S(1)} %copy.66), kind=kOutput, calls=%fused_computation.3.clone.1 | convolution fusion | flops 10485824 | bytes 8388736 | tf_op jit(solution)/shard_map/while/body/eval_jaxpr/mts,cmsqr->cmtqr/dot_general | solution.py:57
  755.3 10.1 %maximum_add_fusion.2 = f32[2,16,2,128,256]{4,3,2,1,0:T(8,128)} fusion(f32[1,16,2,128,256]{4,3,2,1,0:T(8,128)} %add_bitcast_fusion.2, f32[1,16,2,128,256]{4,3,2,1,0:T(8,128)} %subtract_bitcast_fusion.2, f32[2,16,2,128,256]{4,3,2,1,0:T(8,128)} %get-tuple-element.260, pred[]{:T(512)S(6)} %compare.3), kind=kLoop, calls=%fused_computation.1.clone.1 | loop fusion | flops 6291456 | bytes 25165824 | tf_op jit(solution)/shard_map/while/body/eval_jaxpr/add | solution.py:67
  770.8 16.7 %fusion.28 = bf16[2,16,2,128,256]{4,2,3,0,1:T(2,128)(2,1)S(1)} fusion(bf16[2,16,2,128,256]{4,3,2,1,0:T(8,128)(2,1)} %bitcast.98, s32[16,2]{1,0:T(8,128)S(1)} %copy.66), kind=kOutput, calls=%fused_computation.3.clone.1 | convolution fusion | flops 10485824 | bytes 8388736 | tf_op jit(solution)/shard_map/while/body/eval_jaxpr/mts,cmsqr->cmtqr/dot_general | solution.py:57
  799.1 10.1 %maximum_add_fusion.2 = f32[2,16,2,128,256]{4,3,2,1,0:T(8,128)} fusion(f32[1,16,2,128,256]{4,3,2,1,0:T(8,128)} %add_bitcast_fusion.2, f32[1,16,2,128,256]{4,3,2,1,0:T(8,128)} %subtract_bitcast_fusion.2, f32[2,16,2,128,256]{4,3,2,1,0:T(8,128)} %get-tuple-element.260, pred[]{:T(512)S(6)} %compare.3), kind=kLoop, calls=%fused_computation.1.clone.1 | loop fusion | flops 6291456 | bytes 25165824 | tf_op jit(solution)/shard_map/while/body/eval_jaxpr/add | solution.py:67
  814.6 16.7 %fusion.28 = bf16[2,16,2,128,256]{4,2,3,0,1:T(2,128)(2,1)S(1)} fusion(bf16[2,16,2,128,256]{4,3,2,1,0:T(8,128)(2,1)} %bitcast.98, s32[16,2]{1,0:T(8,128)S(1)} %copy.66), kind=kOutput, calls=%fused_computation.3.clone.1 | convolution fusion | flops 10485824 | bytes 8388736 | tf_op jit(solution)/shard_map/while/body/eval_jaxpr/mts,cmsqr->cmtqr/dot_general | solution.py:57
  842.9 10.1 %maximum_add_fusion.2 = f32[2,16,2,128,256]{4,3,2,1,0:T(8,128)} fusion(f32[1,16,2,128,256]{4,3,2,1,0:T(8,128)} %add_bitcast_fusion.2, f32[1,16,2,128,256]{4,3,2,1,0:T(8,128)} %subtract_bitcast_fusion.2, f32[2,16,2,128,256]{4,3,2,1,0:T(8,128)} %get-tuple-element.260, pred[]{:T(512)S(6)} %compare.3), kind=kLoop, calls=%fused_computation.1.clone.1 | loop fusion | flops 6291456 | bytes 25165824 | tf_op jit(solution)/shard_map/while/body/eval_jaxpr/add | solution.py:67
  (103 shorter events, 177.4 us)
Async XLA Ops:
  12.4 470.6 %all-to-all-start = ((bf16[8,2,16,256,256]{4,3,2,1,0:T(8,128)(2,1)}), bf16[8,2,16,256,256]{4,3,2,1,0:T(8,128)(2,1)}, u32[]{:S(2)}, u32[]{:S(2)}) async-start(bf16[8,2,16,256,256]{4,3,2,1,0:T(8,128)(2,1)} %stack.38), calls=%async_computation | async-start | bytes 67108864 | tf_op jit(solution)/shard_map/all_to_all | solution.py:48
  19.5 9.6 %copy-start.4 = (s32[256]{0:T(256)S(1)}, s32[256]{0:T(256)}, u32[]{:S(2)}) copy-start(s32[256]{0:T(256)} %param.13) | copy-start | bytes 3076
  19.5 9.6 %copy-start.3 = (s32[256]{0:T(256)S(1)}, s32[256]{0:T(256)}, u32[]{:S(2)}) copy-start(s32[256]{0:T(256)} %param.12) | copy-start | bytes 3076
  19.5 9.7 %copy-start.2 = (bf16[2,9,16,256]{3,2,1,0:T(8,128)(2,1)S(1)}, bf16[2,9,16,256]{3,2,1,0:T(8,128)(2,1)}, u32[]{:S(2)}) copy-start(bf16[2,9,16,256]{3,2,1,0:T(8,128)(2,1)} %param.11) | copy-start | bytes 442372
  22.6 16.5 %collective-permute-start = (bf16[2,4,256,256]{3,2,1,0:T(8,128)(2,1)}, bf16[2,4,256,256]{3,2,1,0:T(8,128)(2,1)S(1)}, u32[]{:S(2)}, u32[]{:S(2)}) collective-permute-start(bf16[2,4,256,256]{3,2,1,0:T(8,128)(2,1)} %get-tuple-element.178), channel_id=1, source_target_pairs={{0,1},{1,2},{2,3},{3,4},{4,5},{5,6},{6,7},{7,8},{8,9},{9,10},{10,1... | collective-permute-start | bytes 3145736 | tf_op jit(solution)/shard_map/ppermute | solution.py:12
  27.1 20.2 %collective-permute-start.1 = (bf16[2,4,256,256]{3,2,1,0:T(8,128)(2,1)}, bf16[2,4,256,256]{3,2,1,0:T(8,128)(2,1)S(1)}, u32[]{:S(2)}, u32[]{:S(2)}) collective-permute-start(bf16[2,4,256,256]{3,2,1,0:T(8,128)(2,1)} %get-tuple-element.179), channel_id=1, source_target_pairs={{1,0},{2,1},{3,2},{4,3},{5,4},{6,5},{7,6},{8,7},{9,8},{10,9},{11,1... | collective-permute-start | bytes 3145736 | tf_op jit(solution)/shard_map/ppermute | solution.py:15
  47.2 2.3 copy-start
  506.0 347.0 %copy-start.1 = (bf16[1,16,256,256]{3,2,1,0:T(8,128)(2,1)S(1)}, bf16[1,16,256,256]{3,2,1,0:T(8,128)(2,1)}, u32[]{:S(2)}) copy-start(bf16[1,16,256,256]{3,2,1,0:T(8,128)(2,1)} %subtract_convert_fusion) | copy-start | bytes 6291460
